TPU v7x, 256 devices: a whole 4x4x8 slice. The times are simulated.
256 devices in a mesh: sub: 128 (over x, y, z_hi, core), panel: 2 (over z_lo).
Axes of the slice: x: 4, y: 4, z: 8 (z_hi: 4, z_lo: 2; z = z_hi * 2 + z_lo), core: 2. Of those that a mesh axis runs over, the one named last changes fastest.
Arguments:
- solution: float32 [131072, 256], P('sub', 'panel'), may hold values from -6 to 6
- residual: float32 [131072, 256], P('sub', 'panel'), may hold values from -25 to 25
- shadow: float32 [131072, 256], P('sub', 'panel'), may hold values from -120 to 120
- direction: float32 [131072, 256], P('sub', 'panel'), may hold values from -6 to 6
- old_image: float32 [131072, 256], P('sub', 'panel'), may hold values from -6 to 6
- rho_prev: float32 [256], P('panel'), may hold values from 1 to 4
- alpha_prev: float32 [256], P('panel'), may hold values from 0.5 to 2
- omega_prev: float32 [256], P('panel'), may hold values from 0.5 to 2
- lower_inverse: bfloat16 [128, 1792, 1792], P('sub', None, 'panel'), may hold values from -0.4 to 0.4, as said below
- upper_inverse: bfloat16 [128, 1792, 1792], P('sub', None, 'panel'), may hold values from -0.4 to 0.4, as said below
- neighbours: int32 [16, 131072], P(None, 'sub'), may hold values from 0 to 1792, as said below
- edge_weight: float32 [16, 131072], P(None, 'sub'), may hold values from 0.1 to 1
- node_shift: float32 [131072], P('sub'), may hold values from 3 to 12
- send_rows: int32 [128, 2, 384], P('sub'), may hold values from 0 to 1023
Outputs:
- new_solution: float32 [131072, 256], P('sub', 'panel')
- new_residual: float32 [131072, 256], P('sub', 'panel')
- step_alpha: float32 [256], P('panel')
- step_omega: float32 [256], P('panel')
- next_rho: float32 [256], P('panel')
Inputs may be any that keep to these rules, and one draw needn't show every extreme that they name: lower_inverse[s] is zero above its diagonal. upper_inverse[s] is zero below its diagonal. `neighbours`: an entry below 1024 is an owned node, from 1024 a ghost node from the lower neighbour's list, from 1408 one from the upper neighbour's list; 1792 marks an empty slot. send_rows[s, 0] lists the rows of subdomain s that subdomain s - 1 holds as ghosts, send_rows[s, 1] those that subdomain s + 1 holds, modulo 128.
All inputs are finite; a program needn't handle non-finite values.
Results may differ from a plain program's by a relative error of at most 0.0097.
Values may be sent and summed in bfloat16 or wider, within the bound.
A program may use at most 64 MiB of HBM per device.

v0:
```python
import functools
import jax
import jax.numpy as jnp
from jax import lax
from jax.sharding import Mesh
from jax.sharding import PartitionSpec as P

SUB = ("sub_0", "sub_1", "sub_2", "sub_3")
FLOOR_SHARE = 0.3
EPSILON = 1e-06


def padded_2(cells, sides, width):
    for axis, dim in sides:
        count = lax.axis_size(axis)
        head = lax.slice_in_dim(cells, 0, width, axis=dim)
        tail = lax.slice_in_dim(cells, cells.shape[dim] - width, cells.shape[dim], axis=dim)
        cells = jnp.concatenate(
            [
                lax.ppermute(tail, axis, [(i, (i + 1) % count) for i in range(count)]),
                cells,
                lax.ppermute(head, axis, [((i + 1) % count, i) for i in range(count)]),
            ],
            axis=dim,
        )
    return cells


def in_blocks(array, dim, devices):
    lengths = array.shape
    blocks = array.reshape(*lengths[:dim], devices, lengths[dim] // devices, *lengths[dim + 1 :])
    return jnp.moveaxis(blocks, dim, 0)


def sent_and_summed(array, axis, dim):
    devices = lax.axis_size(axis)
    blocks = lax.all_to_all(in_blocks(array, dim, devices), axis, 0, 0, tiled=True)
    return jnp.sum(blocks, axis=0)


def one_axis_at_a_time(array, axes):
    return functools.reduce(lax.psum, axes, array)


def extend(vector, send_rows):
    outgoing = jnp.concatenate([vector[send_rows[0, 0]], vector[send_rows[0, 1]]], axis=0)
    border = send_rows.shape[2]
    padded = padded_2(outgoing, ((SUB, 0),), border)
    return jnp.concatenate([vector, padded[:border], padded[3 * border :]], axis=0)


def operate(vector, send_rows, neighbours, edge_weight, node_shift):
    extended = extend(vector, send_rows)
    ext_rows = extended.shape[0]
    padded = jnp.concatenate([extended, jnp.zeros((1, vector.shape[1]), jnp.float32)], axis=0)
    present = jnp.where(neighbours < ext_rows, edge_weight, 0.0)
    coupled = jnp.sum(present[:, :, None] * padded[neighbours], axis=0)
    diagonal = node_shift + jnp.sum(present, axis=0)
    return diagonal[:, None] * vector - coupled


def precondition(vector, send_rows, factors):
    lower_panel, upper_panel = factors
    own_rows, local_sources = vector.shape
    rounded = extend(vector, send_rows).astype(jnp.bfloat16)
    columns = lax.all_to_all(rounded, "panel", split_axis=0, concat_axis=1, tiled=True)
    inner_part = sent_and_summed(
        jnp.dot(lower_panel, columns, preferred_element_type=jnp.float32), "panel", 0
    ).astype(jnp.bfloat16)
    partial_sum = jnp.dot(upper_panel[:own_rows], inner_part, preferred_element_type=jnp.float32)
    return sent_and_summed(partial_sum, "panel", 1)


def per_device(
    solution,
    residual,
    shadow,
    direction,
    old_image,
    rho_prev,
    alpha_prev,
    omega_prev,
    lower_inverse,
    upper_inverse,
    neighbours,
    edge_weight,
    node_shift,
    send_rows,
):
    node_count = residual.shape[0] * lax.axis_size(SUB)
    factors = (lower_inverse[0], upper_inverse[0])
    opening = (
        one_axis_at_a_time(jnp.sum(shadow * residual, axis=0), SUB),
        one_axis_at_a_time(jnp.sum(shadow * shadow, axis=0), SUB),
    )
    rho_now = opening[0] / node_count
    shadow_square = opening[1] / node_count
    step_beta = rho_now / rho_prev * (alpha_prev / omega_prev)
    new_direction = residual + step_beta * (direction - omega_prev * old_image)
    direction_hat = precondition(new_direction, send_rows, factors)
    image_new = operate(direction_hat, send_rows, neighbours, edge_weight, node_shift)
    second = (
        one_axis_at_a_time(jnp.sum(shadow * image_new, axis=0), SUB),
        one_axis_at_a_time(jnp.sum(image_new * image_new, axis=0), SUB),
    )
    denominator = second[0] / node_count
    image_square = second[1] / node_count
    step_alpha = rho_now / jnp.maximum(
        denominator, FLOOR_SHARE * jnp.sqrt(shadow_square * image_square)
    )
    middle = residual - step_alpha * image_new
    middle_hat = precondition(middle, send_rows, factors)
    tested = operate(middle_hat, send_rows, neighbours, edge_weight, node_shift)
    closing = (
        one_axis_at_a_time(jnp.sum(tested * middle, axis=0), SUB),
        one_axis_at_a_time(jnp.sum(tested * tested, axis=0), SUB),
        one_axis_at_a_time(jnp.sum(shadow * middle, axis=0), SUB),
        one_axis_at_a_time(jnp.sum(shadow * tested, axis=0), SUB),
    )
    step_omega = closing[0] / node_count / (closing[1] / node_count + EPSILON)
    new_residual = middle - step_omega * tested
    next_rho = closing[2] / node_count - step_omega * (closing[3] / node_count)
    new_solution = solution + step_alpha * direction_hat + step_omega * middle_hat
    return (new_solution, new_residual, step_alpha, step_omega, next_rho)


def solution(mesh):
    torus = Mesh(
        mesh.devices.reshape(4, 4, 4, 2, mesh.shape["panel"]),
        ("sub_0", "sub_1", "sub_2", "sub_3", "panel"),
    )
    in_specs = (
        P(SUB, "panel"),
        P(SUB, "panel"),
        P(SUB, "panel"),
        P(SUB, "panel"),
        P(SUB, "panel"),
        P("panel"),
        P("panel"),
        P("panel"),
        P(SUB, None, "panel"),
        P(SUB, None, "panel"),
        P(None, SUB),
        P(None, SUB),
        P(SUB),
        P(SUB, None, None),
    )
    out_specs = (P(SUB, "panel"), P(SUB, "panel"), P("panel"), P("panel"), P("panel"))
    return jax.shard_map(
        per_device, mesh=torus, in_specs=in_specs, out_specs=out_specs, check_vma=False
    )
```

profile of v0, /device:TPU:1, one launch (start us, length us, event | category | flops | bytes accessed | tf_op | source)
XLA Modules:
  0.0 427.7 jit_solution(668824493730074484)
XLA Ops:
  2.1 9.3 %psum.224 = f32[128]{0:T(128)S(1)} all-reduce(f32[128]{0:T(128)S(1)} %multiply_reduce_fusion.9), channel_id=1, replica_groups=mesh['sub_0'=4,'sub_1'=4,'sub_2'=4,'sub_3'=2,'panel'=2] {'sub_0'}, use_global_device_ids=true, to_apply=%region_1.0 | all-reduce | flops 128 | bytes 1024 | tf_op jit(solution)/shard_map/psum | solution.py:42
  11.4 9.0 %psum.225 = f32[128]{0:T(128)S(1)} all-reduce(f32[128]{0:T(128)S(1)} %psum.224), channel_id=1, replica_groups=mesh['sub_0'=4,'sub_1'=4,'sub_2'=4,'sub_3'=2,'panel'=2] {'sub_1'}, use_global_device_ids=true, to_apply=%region_2.0 | all-reduce | flops 128 | bytes 1024 | tf_op jit(solution)/shard_map/psum | solution.py:42
  20.4 12.9 %psum.226 = f32[128]{0:T(128)S(1)} all-reduce(f32[128]{0:T(128)S(1)} %psum.225), channel_id=1, replica_groups=mesh['sub_0'=4,'sub_1'=4,'sub_2'=4,'sub_3'=2,'panel'=2] {'sub_2'}, use_global_device_ids=true, to_apply=%region_3.0 | all-reduce | flops 128 | bytes 1024 | tf_op jit(solution)/shard_map/psum | solution.py:42
  33.3 8.6 %psum.227 = f32[128]{0:T(128)S(1)} all-reduce(f32[128]{0:T(128)S(1)} %psum.226), channel_id=1, replica_groups=mesh['sub_0'=4,'sub_1'=4,'sub_2'=4,'sub_3'=2,'panel'=2] {'sub_3'}, use_global_device_ids=true, to_apply=%region_4.0 | all-reduce | flops 128 | bytes 1024 | tf_op jit(solution)/shard_map/psum | solution.py:42
  49.2 6.3 %collective-permute-done.1 = bf16[384,128]{1,0:T(8,128)(2,1)S(1)} collective-permute-done((bf16[384,128]{1,0:T(8,128)(2,1)}, bf16[384,128]{1,0:T(8,128)(2,1)S(1)}, u32[]{:S(2)}, u32[]{:S(2)}) %collective-permute-start.1) | collective-permute-done | bytes 98336 | tf_op jit(solution)/shard_map/ppermute | solution.py:22
  59.1 8.5 %all_to_all.52 = bf16[2,896,128]{1,2,0:T(8,128)(2,1)S(1)} all-to-all(bf16[2,896,128]{1,2,0:T(8,128)(2,1)} %copy.21), channel_id=1, replica_groups=mesh['sub_0'=4,'sub_1'=4,'sub_2'=4,'sub_3'=2,'panel'=2] {'panel'}, dimensions={0} | all-to-all | bytes 917504 | tf_op jit(solution)/shard_map/all_to_all | solution.py:66
  69.0 19.2 %all_to_all.53 = f32[2,896,256]{1,2,0:T(8,128)} all-to-all(f32[2,896,256]{1,2,0:T(8,128)S(1)} %bitcast.54), channel_id=1, replica_groups=mesh['sub_0'=4,'sub_1'=4,'sub_2'=4,'sub_3'=2,'panel'=2] {'panel'}, dimensions={0} | all-to-all | bytes 3670016 | tf_op jit(solution)/shard_map/all_to_all | solution.py:37
  88.1 2.5 reduce_sum.141
  90.7 3.5 fusion.6
  94.1 4.4 %all-to-all-start.2 = ((f32[2,1024,128]{1,2,0:T(8,128)}), f32[2,1024,128]{1,2,0:T(8,128)}, u32[]{:S(2)}, u32[]{:S(2)}) async-start(f32[2,1024,128]{1,2,0:T(8,128)} %bitcast.62), calls=%async_computation.2 | async-start | bytes 2097152 | tf_op jit(solution)/shard_map/all_to_all | solution.py:37
  98.6 8.2 %all-to-all-done.2 = f32[2,1024,128]{1,2,0:T(8,128)} async-done(((f32[2,1024,128]{1,2,0:T(8,128)}), f32[2,1024,128]{1,2,0:T(8,128)}, u32[]{:S(2)}, u32[]{:S(2)}) %all-to-all-start.2) | async-done | bytes 1048608 | tf_op jit(solution)/shard_map/all_to_all | solution.py:37
  106.8 2.1 reduce_sum.142
  111.0 2.7 gather_fusion.3
  113.7 2.6 gather_fusion.2
  116.3 12.4 %collective-permute-start.2 = (f32[384,128]{1,0:T(8,128)}, f32[384,128]{1,0:T(8,128)S(1)}, u32[]{:S(2)}, u32[]{:S(2)}) collective-permute-start(f32[384,128]{1,0:T(8,128)} %gather_fusion.2), channel_id=1, source_target_pairs={{0,2},{2,4},{4,6},{6,8},{8,10},{10,12},{12,14},{14,16},{16,18},{18... | collective-permute-start | bytes 589832 | tf_op jit(solution)/shard_map/ppermute | solution.py:20
  128.8 4.8 %collective-permute-done.2 = f32[384,128]{1,0:T(8,128)S(1)} collective-permute-done((f32[384,128]{1,0:T(8,128)}, f32[384,128]{1,0:T(8,128)S(1)}, u32[]{:S(2)}, u32[]{:S(2)}) %collective-permute-start.2) | collective-permute-done | bytes 196640 | tf_op jit(solution)/shard_map/ppermute | solution.py:20
  133.6 2.7 collective-permute-done.3
  136.3 2.3 maximum_maximum_fusion
  138.7 55.6 %gather_fusion.4 = f32[16384,128]{1,0:T(8,128)} fusion(f32[1793,128]{1,0:T(8,128)} %maximum_maximum_fusion, s32[16384]{0:T(1024)S(1)} %broadcast_clamp_fusion), kind=kCustom, calls=%fused_computation.4 | custom fusion | bytes 16842752 | tf_op jit(solution)/shard_map/gather | solution.py:57
  194.3 5.3 %multiply_reduce_fusion.1 = f32[1024,128]{1,0:T(8,128)S(1)} fusion(f32[16,1024,128]{2,1,0:T(8,128)} %bitcast.53, f32[16,1024]{1,0:T(8,128)S(1)} %get-tuple-element.49), kind=kLoop, calls=%fused_computation.11 | loop fusion | flops 4063232 | bytes 8978432 | tf_op jit(solution)/shard_map/reduce_sum | solution.py:57
  200.6 6.2 %all-reduce.5 = (f32[128]{0:T(128)S(1)}, f32[128]{0:T(128)S(1)}, f32[128]{0:T(128)S(1)}) all-reduce(f32[128]{0:T(128)S(1)} %get-tuple-element.10, f32[128]{0:T(128)S(1)} %get-tuple-element.11, f32[128]{0:T(128)S(1)} %get-tuple-element.9), channel_id=1, replica_groups=mesh['sub_0'=4,'sub_1'=4,'sub_2'=4,'sub_3'=2,'panel'=2] {'sub_0'}, use_global_device_ids=true, to_apply=%region_20.21 | all-reduce | flops 384 | bytes 3072 | tf_op jit(solution)/shard_map/psum | solution.py:42
  206.8 6.0 %all-reduce.3 = (f32[128]{0:T(128)S(1)}, f32[128]{0:T(128)S(1)}, f32[128]{0:T(128)S(1)}) all-reduce(f32[128]{0:T(128)S(1)} %get-tuple-element.32, f32[128]{0:T(128)S(1)} %get-tuple-element.33, f32[128]{0:T(128)S(1)} %get-tuple-element.34), channel_id=1, replica_groups=mesh['sub_0'=4,'sub_1'=4,'sub_2'=4,'sub_3'=2,'panel'=2] {'sub_1'}, use_global_device_ids=true, to_apply=%region_21.22 | all-reduce | flops 384 | bytes 3072 | tf_op jit(solution)/shard_map/psum | solution.py:42
  212.8 16.5 %all-reduce.1 = (f32[128]{0:T(128)S(1)}, f32[128]{0:T(128)S(1)}, f32[128]{0:T(128)S(1)}) all-reduce(f32[128]{0:T(128)S(1)} %get-tuple-element.25, f32[128]{0:T(128)S(1)} %get-tuple-element.26, f32[128]{0:T(128)S(1)} %get-tuple-element.27), channel_id=1, replica_groups=mesh['sub_0'=4,'sub_1'=4,'sub_2'=4,'sub_3'=2,'panel'=2] {'sub_2'}, use_global_device_ids=true, to_apply=%region_22.23 | all-reduce | flops 384 | bytes 3072 | tf_op jit(solution)/shard_map/psum | solution.py:42
  229.3 2.5 all-reduce.7
  232.3 2.1 fusion.15
  234.3 2.8 gather_fusion.6
  237.2 2.7 gather_fusion.5
  243.2 4.0 collective-permute-done.5
  250.0 8.5 %all_to_all.54 = bf16[2,896,128]{1,2,0:T(8,128)(2,1)S(1)} all-to-all(bf16[2,896,128]{1,2,0:T(8,128)(2,1)} %copy.29), channel_id=1, replica_groups=mesh['sub_0'=4,'sub_1'=4,'sub_2'=4,'sub_3'=2,'panel'=2] {'panel'}, dimensions={0} | all-to-all | bytes 917504 | tf_op jit(solution)/shard_map/all_to_all | solution.py:66
  259.8 19.9 %all_to_all.55 = f32[2,896,256]{1,2,0:T(8,128)} all-to-all(f32[2,896,256]{1,2,0:T(8,128)S(1)} %bitcast.55), channel_id=1, replica_groups=mesh['sub_0'=4,'sub_1'=4,'sub_2'=4,'sub_3'=2,'panel'=2] {'panel'}, dimensions={0} | all-to-all | bytes 3670016 | tf_op jit(solution)/shard_map/all_to_all | solution.py:37
  279.8 2.5 reduce_sum.147
  282.3 2.4 fusion.4
  284.7 11.5 %all_to_all.56 = f32[2,1024,128]{1,2,0:T(8,128)} all-to-all(f32[2,1024,128]{1,2,0:T(8,128)S(1)} %bitcast.63), channel_id=1, replica_groups=mesh['sub_0'=4,'sub_1'=4,'sub_2'=4,'sub_3'=2,'panel'=2] {'panel'}, dimensions={0} | all-to-all | bytes 2097152 | tf_op jit(solution)/shard_map/all_to_all | solution.py:37
  296.2 2.2 reduce_sum.148
  298.3 2.1 copy.32
  300.4 2.6 gather_fusion.8
  303.1 2.7 gather_fusion.7
  305.7 14.1 %collective-permute-start.6 = (f32[384,128]{1,0:T(8,128)}, f32[384,128]{1,0:T(8,128)S(1)}, u32[]{:S(2)}, u32[]{:S(2)}) collective-permute-start(f32[384,128]{1,0:T(8,128)} %gather_fusion.7), channel_id=1, source_target_pairs={{0,2},{2,4},{4,6},{6,8},{8,10},{10,12},{12,14},{14,16},{16,18},{18... | collective-permute-start | bytes 589832 | tf_op jit(solution)/shard_map/ppermute | solution.py:20
  319.8 3.0 collective-permute-done.6
  322.8 5.1 %collective-permute-done.7 = f32[384,128]{1,0:T(8,128)S(1)} collective-permute-done((f32[384,128]{1,0:T(8,128)}, f32[384,128]{1,0:T(8,128)S(1)}, u32[]{:S(2)}, u32[]{:S(2)}) %collective-permute-start.7) | collective-permute-done | bytes 196640 | tf_op jit(solution)/shard_map/ppermute | solution.py:22
  327.9 2.3 maximum_maximum_fusion.1
  330.2 55.6 %gather_fusion.9 = f32[16384,128]{1,0:T(8,128)} fusion(f32[1793,128]{1,0:T(8,128)} %maximum_maximum_fusion.1, s32[16384]{0:T(1024)S(1)} %copy-done.7), kind=kCustom, calls=%fused_computation.9 | custom fusion | bytes 16842752 | tf_op jit(solution)/shard_map/gather | solution.py:57
  385.8 5.4 %multiply_reduce_fusion = f32[1024,128]{1,0:T(8,128)S(1)} fusion(f32[16,1024,128]{2,1,0:T(8,128)} %bitcast.52, f32[16,1024]{1,0:T(8,128)S(1)} %get-tuple-element.49), kind=kLoop, calls=%fused_computation.10 | loop fusion | flops 4063232 | bytes 8978432 | tf_op jit(solution)/shard_map/reduce_sum | solution.py:57
  392.2 8.1 %all-reduce.4 = (f32[128]{0:T(128)S(1)}, f32[128]{0:T(128)S(1)}, f32[128]{0:T(128)S(1)}, f32[128]{0:T(128)S(1)}) all-reduce(f32[128]{0:T(128)S(1)} %get-tuple-element.8, f32[128]{0:T(128)S(1)} %get-tuple-element.6, f32[128]{0:T(128)S(1)} %get-tuple-element.7, ...), channel_id=1, replica_groups=mesh['sub_0'=4,'sub_1'=4,'sub_2'=4,'sub_3'=2,'panel'=2] {'sub_0'}, use_global_device_ids=true, to_apply=%region_33.34 | all-reduce | flops 512 | bytes 4096 | tf_op jit(solution)/shard_map/psum | solution.py:42
  400.3 8.1 %all-reduce.2 = (f32[128]{0:T(128)S(1)}, f32[128]{0:T(128)S(1)}, f32[128]{0:T(128)S(1)}, f32[128]{0:T(128)S(1)}) all-reduce(f32[128]{0:T(128)S(1)} %get-tuple-element.28, f32[128]{0:T(128)S(1)} %get-tuple-element.29, f32[128]{0:T(128)S(1)} %get-tuple-element.30, ...), channel_id=1, replica_groups=mesh['sub_0'=4,'sub_1'=4,'sub_2'=4,'sub_3'=2,'panel'=2] {'sub_1'}, use_global_device_ids=true, to_apply=%region_34.35 | all-reduce | flops 512 | bytes 4096 | tf_op jit(solution)/shard_map/psum | solution.py:42
  408.4 11.4 %all-reduce = (f32[128]{0:T(128)S(1)}, f32[128]{0:T(128)S(1)}, f32[128]{0:T(128)S(1)}, f32[128]{0:T(128)S(1)}) all-reduce(f32[128]{0:T(128)S(1)} %get-tuple-element.21, f32[128]{0:T(128)S(1)} %get-tuple-element.22, f32[128]{0:T(128)S(1)} %get-tuple-element.23, ...), channel_id=1, replica_groups=mesh['sub_0'=4,'sub_1'=4,'sub_2'=4,'sub_3'=2,'panel'=2] {'sub_2'}, use_global_device_ids=true, to_apply=%region_35.36 | all-reduce | flops 512 | bytes 4096 | tf_op jit(solution)/shard_map/psum | solution.py:42
  419.9 4.5 %all-reduce.6 = (f32[128]{0:T(128)S(1)}, f32[128]{0:T(128)S(1)}, f32[128]{0:T(128)S(1)}, f32[128]{0:T(128)S(1)}) all-reduce(f32[128]{0:T(128)S(1)} %get-tuple-element.14, f32[128]{0:T(128)S(1)} %get-tuple-element.15, f32[128]{0:T(128)S(1)} %get-tuple-element.16, ...), channel_id=1, replica_groups=mesh['sub_0'=4,'sub_1'=4,'sub_2'=4,'sub_3'=2,'panel'=2] {'sub_3'}, use_global_device_ids=true, to_apply=%region_36.37 | all-reduce | flops 512 | bytes 4096 | tf_op jit(solution)/shard_map/psum | solution.py:42
  424.9 2.8 multiply_subtract_fusion
  (71 shorter events, 26.4 us)
Async XLA Ops:
  0.6 67.0 %copy-start = (bf16[1,1792,896]{2,1,0:T(8,128)(2,1)S(1)}, bf16[1,1792,896]{2,1,0:T(8,128)(2,1)}, u32[]{:S(2)}) copy-start(bf16[1,1792,896]{2,1,0:T(8,128)(2,1)} %param.22) | copy-start | bytes 9633796
  41.9 27.0 %copy-start.16 = (f32[128]{0:T(128)}, f32[128]{0:T(128)S(1)}, u32[]{:S(2)}) copy-start(f32[128]{0:T(128)S(1)} %psum.227) | copy-start | bytes 1540
  46.7 2.4 collective-permute-start
  46.9 64.1 %copy-start.10 = (s32[1024]{0:T(1024)}, s32[1024]{0:T(1024)S(1)}, u32[]{:S(2)}) copy-start(s32[1024]{0:T(1024)S(1)} %pad_clamp_fusion) | copy-start | bytes 12292
  48.8 6.6 %collective-permute-start.1 = (bf16[384,128]{1,0:T(8,128)(2,1)}, bf16[384,128]{1,0:T(8,128)(2,1)S(1)}, u32[]{:S(2)}, u32[]{:S(2)}) collective-permute-start(bf16[384,128]{1,0:T(8,128)(2,1)} %gather_fusion.1), channel_id=1, source_target_pairs={{2,0},{4,2},{6,4},{8,6},{10,8},{12,10},{14,12},{16,14},{18,16},{20... | collective-permute-start | bytes 294920 | tf_op jit(solution)/shard_map/ppermute | solution.py:22
  90.7 7.9 %copy-start.8 = (s32[16,1024]{1,0:T(8,128)S(1)}, s32[16,1024]{1,0:T(8,128)}, u32[]{:S(2)}) copy-start(s32[16,1024]{1,0:T(8,128)} %param.24) | copy-start | bytes 196612
  94.1 12.7 %all-to-all-start.2 = ((f32[2,1024,128]{1,2,0:T(8,128)}), f32[2,1024,128]{1,2,0:T(8,128)}, u32[]{:S(2)}, u32[]{:S(2)}) async-start(f32[2,1024,128]{1,2,0:T(8,128)} %bitcast.62), calls=%async_computation.2 | async-start | bytes 2097152 | tf_op jit(solution)/shard_map/all_to_all | solution.py:37
  98.6 30.2 %copy-start.9 = (f32[16,1024]{1,0:T(8,128)S(1)}, f32[16,1024]{1,0:T(8,128)}, u32[]{:S(2)}) copy-start(f32[16,1024]{1,0:T(8,128)} %param.25) | copy-start | bytes 196612
  98.6 40.1 %copy-start.6 = (s32[16384]{0:T(1024)}, s32[16384]{0:T(1024)S(1)}, u32[]{:S(2)}) copy-start(s32[16384]{0:T(1024)S(1)} %broadcast_clamp_fusion) | copy-start | bytes 196612
  98.6 30.2 %copy-start.14 = (f32[1024]{0:T(1024)S(1)}, f32[1024]{0:T(1024)}, u32[]{:S(2)}) copy-start(f32[1024]{0:T(1024)} %param.26) | copy-start | bytes 12292
  116.3 17.3 %collective-permute-start.2 = (f32[384,128]{1,0:T(8,128)}, f32[384,128]{1,0:T(8,128)S(1)}, u32[]{:S(2)}, u32[]{:S(2)}) collective-permute-start(f32[384,128]{1,0:T(8,128)} %gather_fusion.2), channel_id=1, source_target_pairs={{0,2},{2,4},{4,6},{6,8},{8,10},{10,12},{12,14},{14,16},{16,18},{18... | collective-permute-start | bytes 589832 | tf_op jit(solution)/shard_map/ppermute | solution.py:20
  128.8 7.6 %collective-permute-start.3 = (f32[384,128]{1,0:T(8,128)}, f32[384,128]{1,0:T(8,128)S(1)}, u32[]{:S(2)}, u32[]{:S(2)}) collective-permute-start(f32[384,128]{1,0:T(8,128)} %gather_fusion.3), channel_id=1, source_target_pairs={{2,0},{4,2},{6,4},{8,6},{10,8},{12,10},{14,12},{16,14},{18,16},{20... | collective-permute-start | bytes 589832 | tf_op jit(solution)/shard_map/ppermute | solution.py:22
  194.3 5.3 %copy-start.1 = (f32[1024,128]{1,0:T(8,128)S(1)}, f32[1024,128]{1,0:T(8,128)}, u32[]{:S(2)}) copy-start(f32[1024,128]{1,0:T(8,128)} %copy.24) | copy-start | bytes 1572868
  194.3 5.4 %copy-start.4 = (f32[1024,128]{1,0:T(8,128)S(1)}, f32[1024,128]{1,0:T(8,128)}, u32[]{:S(2)}) copy-start(f32[1024,128]{1,0:T(8,128)} %param.16) | copy-start | bytes 1572868
  194.3 37.5 %copy-start.17 = (f32[128]{0:T(128)S(1)}, f32[128]{0:T(128)}, u32[]{:S(2)}) copy-start(f32[128]{0:T(128)} %copy-done.16) | copy-start | bytes 1540
  231.8 0.5 copy-start.12
  239.8 3.4 collective-permute-start.4
  241.2 6.0 %collective-permute-start.5 = (bf16[384,128]{1,0:T(8,128)(2,1)}, bf16[384,128]{1,0:T(8,128)(2,1)S(1)}, u32[]{:S(2)}, u32[]{:S(2)}) collective-permute-start(bf16[384,128]{1,0:T(8,128)(2,1)} %gather_fusion.6), channel_id=1, source_target_pairs={{2,0},{4,2},{6,4},{8,6},{10,8},{12,10},{14,12},{16,14},{18,16},{20... | collective-permute-start | bytes 294920 | tf_op jit(solution)/shard_map/ppermute | solution.py:22
  284.7 15.7 %copy-start.11 = (s32[1024]{0:T(1024)S(1)}, s32[1024]{0:T(1024)}, u32[]{:S(2)}) copy-start(s32[1024]{0:T(1024)} %copy-done.10) | copy-start | bytes 12292
  298.3 31.9 %copy-start.7 = (s32[16384]{0:T(1024)S(1)}, s32[16384]{0:T(1024)}, u32[]{:S(2)}) copy-start(s32[16384]{0:T(1024)} %copy-done.6) | copy-start | bytes 196612
  305.7 17.1 %collective-permute-start.6 = (f32[384,128]{1,0:T(8,128)}, f32[384,128]{1,0:T(8,128)S(1)}, u32[]{:S(2)}, u32[]{:S(2)}) collective-permute-start(f32[384,128]{1,0:T(8,128)} %gather_fusion.7), channel_id=1, source_target_pairs={{0,2},{2,4},{4,6},{6,8},{8,10},{10,12},{12,14},{14,16},{16,18},{18... | collective-permute-start | bytes 589832 | tf_op jit(solution)/shard_map/ppermute | solution.py:20
  319.8 8.0 %collective-permute-start.7 = (f32[384,128]{1,0:T(8,128)}, f32[384,128]{1,0:T(8,128)S(1)}, u32[]{:S(2)}, u32[]{:S(2)}) collective-permute-start(f32[384,128]{1,0:T(8,128)} %gather_fusion.8), channel_id=1, source_target_pairs={{2,0},{4,2},{6,4},{8,6},{10,8},{12,10},{14,12},{16,14},{18,16},{20... | collective-permute-start | bytes 589832 | tf_op jit(solution)/shard_map/ppermute | solution.py:22
  385.8 5.4 %copy-start.2 = (f32[1024,128]{1,0:T(8,128)S(1)}, f32[1024,128]{1,0:T(8,128)}, u32[]{:S(2)}) copy-start(f32[1024,128]{1,0:T(8,128)} %copy.32) | copy-start | bytes 1572868
  385.8 5.4 %copy-start.3 = (f32[1024,128]{1,0:T(8,128)S(1)}, f32[1024,128]{1,0:T(8,128)}, u32[]{:S(2)}) copy-start(f32[1024,128]{1,0:T(8,128)} %get-tuple-element.46) | copy-start | bytes 1572868
  385.8 5.4 %copy-start.5 = (f32[1024,128]{1,0:T(8,128)S(1)}, f32[1024,128]{1,0:T(8,128)}, u32[]{:S(2)}) copy-start(f32[1024,128]{1,0:T(8,128)} %param.16) | copy-start | bytes 1572868
  385.8 39.1 %copy-start.13 = (f32[128]{0:T(128)S(1)}, f32[128]{0:T(128)}, u32[]{:S(2)}) copy-start(f32[128]{0:T(128)} %copy-done.12) | copy-start | bytes 1540
  424.9 2.8 copy-start.15
where the time goes:
time: 429 us; the launch traced here: 428 us
  blocking collectives  171 us (40%)
  local copies, waits for them, and re-layouts  140 us (33%)
  other arithmetic  39.1 us (9%)
  waiting for transfers between devices  36 us (8%)
  starting transfers between devices  32.9 us (8%)
  matrix products  8.16 us (2%)
    gather x2, local copies, waits for them, and re-layouts, operate(): coupled = jnp.sum(present[:, :, None] * padded[neighbours], axis=0)  111 us
    psum x12, blocking collectives, one_axis_at_a_time(): return functools.reduce(lax.psum, axes, array)  103 us
    all_to_all x3, blocking collectives, sent_and_summed(): lax.all_to_all(in_blocks(array, dim, devices), axis, 0, 0, tiled=True)  50.6 us
    ppermute x4, starting transfers between devices, padded_2(): lax.ppermute(tail, axis, [(i, (i + 1) % count) for i in range(count)])  28.1 us
    ppermute x4, waiting for transfers between devices, padded_2(): lax.ppermute(head, axis, [((i + 1) % count, i) for i in range(count)])  18.1 us
    all_to_all x2, blocking collectives, precondition(): lax.all_to_all(rounded, 'panel', split_axis=0, concat_axis=1, tiled=True)  17.1 us
    reduce_sum x2, other arithmetic, operate(): coupled = jnp.sum(present[:, :, None] * padded[neighbours], axis=0)  10.7 us
    gather x4, local copies, waits for them, and re-layouts, extend(): vector[send_rows[0, 0]]  10 us
  transfers between devices with their start and end apart: 9, of which 8 were waited for; matrix products, arithmetic and copies ran while one was open for 0% of the time, Pallas kernels for 0%

commit v1 on v0

--- a/solution.py
+++ b/solution.py
@@ -63,7 +63,12 @@
     lower_panel, upper_panel = factors
     own_rows, local_sources = vector.shape
     rounded = extend(vector, send_rows).astype(jnp.bfloat16)
-    columns = lax.all_to_all(rounded, "panel", split_axis=0, concat_axis=1, tiled=True)
+    columns = jnp.concatenate(
+        jax.lax.all_to_all(
+            jnp.stack(jnp.split(rounded, jax.lax.axis_size("panel"), axis=0)), "panel", 0, 0
+        ),
+        axis=1,
+    )
     inner_part = sent_and_summed(
         jnp.dot(lower_panel, columns, preferred_element_type=jnp.float32), "panel", 0
     ).astype(jnp.bfloat16)

time: 429 us -> 428 us (level)
  no operation moved by 1% of the time
where the time goes in v1:
time: 428 us; the launch traced here: 426 us
  blocking collectives  168 us (39%)
  local copies, waits for them, and re-layouts  140 us (33%)
  other arithmetic  37.7 us (9%)
  waiting for transfers between devices  36.3 us (8%)
  starting transfers between devices  32.5 us (8%)
  matrix products  10.1 us (2%)
    gather x2, local copies, waits for them, and re-layouts, operate(): coupled = jnp.sum(present[:, :, None] * padded[neighbours], axis=0)  111 us
    psum x12, blocking collectives, one_axis_at_a_time(): return functools.reduce(lax.psum, axes, array)  102 us
    all_to_all x3, blocking collectives, sent_and_summed(): lax.all_to_all(in_blocks(array, dim, devices), axis, 0, 0, tiled=True)  50.5 us
    ppermute x4, starting transfers between devices, padded_2(): lax.ppermute(tail, axis, [(i, (i + 1) % count) for i in range(count)])  27.8 us
    ppermute x4, waiting for transfers between devices, padded_2(): lax.ppermute(head, axis, [((i + 1) % count, i) for i in range(count)])  18.1 us
    all_to_all x2, blocking collectives, precondition(): jax.lax.all_to_all(jnp.stack(jnp.split(rounded, jax.lax.axis_size('panel'...  16.4 us
    reduce_sum x2, other arithmetic, operate(): coupled = jnp.sum(present[:, :, None] * padded[neighbours], axis=0)  10.7 us
    gather x4, local copies, waits for them, and re-layouts, extend(): vector[send_rows[0, 0]]  10 us
  transfers between devices with their start and end apart: 9, of which 8 were waited for; matrix products, arithmetic and copies ran while one was open for 0% of the time, Pallas kernels for 0%

profile of v1, /device:TPU:1, one launch (start us, length us, event | category | flops | bytes accessed | tf_op | source)
XLA Modules:
  0.0 426.0 jit_solution(7439653412749846039)
XLA Ops:
  2.1 9.3 %psum.224 = f32[128]{0:T(128)S(1)} all-reduce(f32[128]{0:T(128)S(1)} %multiply_reduce_fusion.9), channel_id=1, replica_groups=mesh['sub_0'=4,'sub_1'=4,'sub_2'=4,'sub_3'=2,'panel'=2] {'sub_0'}, use_global_device_ids=true, to_apply=%region_1.0 | all-reduce | flops 128 | bytes 1024 | tf_op jit(solution)/shard_map/psum | solution.py:42
  11.4 9.0 %psum.225 = f32[128]{0:T(128)S(1)} all-reduce(f32[128]{0:T(128)S(1)} %psum.224), channel_id=1, replica_groups=mesh['sub_0'=4,'sub_1'=4,'sub_2'=4,'sub_3'=2,'panel'=2] {'sub_1'}, use_global_device_ids=true, to_apply=%region_2.0 | all-reduce | flops 128 | bytes 1024 | tf_op jit(solution)/shard_map/psum | solution.py:42
  20.4 12.9 %psum.226 = f32[128]{0:T(128)S(1)} all-reduce(f32[128]{0:T(128)S(1)} %psum.225), channel_id=1, replica_groups=mesh['sub_0'=4,'sub_1'=4,'sub_2'=4,'sub_3'=2,'panel'=2] {'sub_2'}, use_global_device_ids=true, to_apply=%region_3.0 | all-reduce | flops 128 | bytes 1024 | tf_op jit(solution)/shard_map/psum | solution.py:42
  33.3 8.6 %psum.227 = f32[128]{0:T(128)S(1)} all-reduce(f32[128]{0:T(128)S(1)} %psum.226), channel_id=1, replica_groups=mesh['sub_0'=4,'sub_1'=4,'sub_2'=4,'sub_3'=2,'panel'=2] {'sub_3'}, use_global_device_ids=true, to_apply=%region_4.0 | all-reduce | flops 128 | bytes 1024 | tf_op jit(solution)/shard_map/psum | solution.py:42
  49.2 6.3 %collective-permute-done.1 = bf16[384,128]{1,0:T(8,128)(2,1)S(1)} collective-permute-done((bf16[384,128]{1,0:T(8,128)(2,1)}, bf16[384,128]{1,0:T(8,128)(2,1)S(1)}, u32[]{:S(2)}, u32[]{:S(2)}) %collective-permute-start.1) | collective-permute-done | bytes 98336 | tf_op jit(solution)/shard_map/ppermute | solution.py:22
  56.4 8.2 %all_to_all.30 = bf16[2,896,128]{2,1,0:T(8,128)(2,1)} all-to-all(bf16[2,896,128]{2,1,0:T(8,128)(2,1)S(1)} %pad_maximum_fusion), channel_id=1, replica_groups=mesh['sub_0'=4,'sub_1'=4,'sub_2'=4,'sub_3'=2,'panel'=2] {'panel'}, dimensions={0} | all-to-all | bytes 917504 | tf_op jit(solution)/shard_map/all_to_all | solution.py:67
  66.6 2.2 fusion.2
  68.9 19.2 %all_to_all.31 = f32[2,896,256]{1,2,0:T(8,128)} all-to-all(f32[2,896,256]{1,2,0:T(8,128)S(1)} %bitcast.58), channel_id=1, replica_groups=mesh['sub_0'=4,'sub_1'=4,'sub_2'=4,'sub_3'=2,'panel'=2] {'panel'}, dimensions={0} | all-to-all | bytes 3670016 | tf_op jit(solution)/shard_map/all_to_all | solution.py:37
  88.1 2.5 reduce_sum.141
  90.6 3.5 fusion.6
  94.0 4.4 %all-to-all-start.2 = ((f32[2,1024,128]{1,2,0:T(8,128)}), f32[2,1024,128]{1,2,0:T(8,128)}, u32[]{:S(2)}, u32[]{:S(2)}) async-start(f32[2,1024,128]{1,2,0:T(8,128)} %bitcast.66), calls=%async_computation.2 | async-start | bytes 2097152 | tf_op jit(solution)/shard_map/all_to_all | solution.py:37
  98.6 8.2 %all-to-all-done.2 = f32[2,1024,128]{1,2,0:T(8,128)} async-done(((f32[2,1024,128]{1,2,0:T(8,128)}), f32[2,1024,128]{1,2,0:T(8,128)}, u32[]{:S(2)}, u32[]{:S(2)}) %all-to-all-start.2) | async-done | bytes 1048608 | tf_op jit(solution)/shard_map/all_to_all | solution.py:37
  106.8 2.1 reduce_sum.142
  110.9 2.7 gather_fusion.3
  113.6 2.6 gather_fusion.2
  116.3 12.4 %collective-permute-start.2 = (f32[384,128]{1,0:T(8,128)}, f32[384,128]{1,0:T(8,128)S(1)}, u32[]{:S(2)}, u32[]{:S(2)}) collective-permute-start(f32[384,128]{1,0:T(8,128)} %gather_fusion.2), channel_id=1, source_target_pairs={{0,2},{2,4},{4,6},{6,8},{8,10},{10,12},{12,14},{14,16},{16,18},{18... | collective-permute-start | bytes 589832 | tf_op jit(solution)/shard_map/ppermute | solution.py:20
  128.7 5.0 %collective-permute-done.2 = f32[384,128]{1,0:T(8,128)S(1)} collective-permute-done((f32[384,128]{1,0:T(8,128)}, f32[384,128]{1,0:T(8,128)S(1)}, u32[]{:S(2)}, u32[]{:S(2)}) %collective-permute-start.2) | collective-permute-done | bytes 196640 | tf_op jit(solution)/shard_map/ppermute | solution.py:20
  133.8 2.5 collective-permute-done.3
  136.3 2.3 maximum_maximum_fusion
  138.6 55.6 %gather_fusion.4 = f32[16384,128]{1,0:T(8,128)} fusion(f32[1793,128]{1,0:T(8,128)} %maximum_maximum_fusion, s32[16384]{0:T(1024)S(1)} %broadcast_clamp_fusion), kind=kCustom, calls=%fused_computation.4 | custom fusion | bytes 16842752 | tf_op jit(solution)/shard_map/gather | solution.py:57
  194.2 5.3 %multiply_reduce_fusion.1 = f32[1024,128]{1,0:T(8,128)S(1)} fusion(f32[16,1024,128]{2,1,0:T(8,128)} %bitcast.57, f32[16,1024]{1,0:T(8,128)S(1)} %get-tuple-element.49), kind=kLoop, calls=%fused_computation.11 | loop fusion | flops 4063232 | bytes 8978432 | tf_op jit(solution)/shard_map/reduce_sum | solution.py:57
  200.6 6.2 %all-reduce.5 = (f32[128]{0:T(128)S(1)}, f32[128]{0:T(128)S(1)}, f32[128]{0:T(128)S(1)}) all-reduce(f32[128]{0:T(128)S(1)} %get-tuple-element.10, f32[128]{0:T(128)S(1)} %get-tuple-element.11, f32[128]{0:T(128)S(1)} %get-tuple-element.9), channel_id=1, replica_groups=mesh['sub_0'=4,'sub_1'=4,'sub_2'=4,'sub_3'=2,'panel'=2] {'sub_0'}, use_global_device_ids=true, to_apply=%region_20.21 | all-reduce | flops 384 | bytes 3072 | tf_op jit(solution)/shard_map/psum | solution.py:42
  206.8 6.0 %all-reduce.3 = (f32[128]{0:T(128)S(1)}, f32[128]{0:T(128)S(1)}, f32[128]{0:T(128)S(1)}) all-reduce(f32[128]{0:T(128)S(1)} %get-tuple-element.32, f32[128]{0:T(128)S(1)} %get-tuple-element.33, f32[128]{0:T(128)S(1)} %get-tuple-element.34), channel_id=1, replica_groups=mesh['sub_0'=4,'sub_1'=4,'sub_2'=4,'sub_3'=2,'panel'=2] {'sub_1'}, use_global_device_ids=true, to_apply=%region_21.22 | all-reduce | flops 384 | bytes 3072 | tf_op jit(solution)/shard_map/psum | solution.py:42
  212.8 16.4 %all-reduce.1 = (f32[128]{0:T(128)S(1)}, f32[128]{0:T(128)S(1)}, f32[128]{0:T(128)S(1)}) all-reduce(f32[128]{0:T(128)S(1)} %get-tuple-element.25, f32[128]{0:T(128)S(1)} %get-tuple-element.26, f32[128]{0:T(128)S(1)} %get-tuple-element.27), channel_id=1, replica_groups=mesh['sub_0'=4,'sub_1'=4,'sub_2'=4,'sub_3'=2,'panel'=2] {'sub_2'}, use_global_device_ids=true, to_apply=%region_22.23 | all-reduce | flops 384 | bytes 3072 | tf_op jit(solution)/shard_map/psum | solution.py:42
  229.2 2.5 all-reduce.7
  234.2 2.8 gather_fusion.6
  237.0 2.7 gather_fusion.5
  242.8 4.2 collective-permute-done.5
  247.1 8.2 %all_to_all.32 = bf16[2,896,128]{2,1,0:T(8,128)(2,1)} all-to-all(bf16[2,896,128]{2,1,0:T(8,128)(2,1)S(1)} %pad_maximum_fusion.1), channel_id=1, replica_groups=mesh['sub_0'=4,'sub_1'=4,'sub_2'=4,'sub_3'=2,'panel'=2] {'panel'}, dimensions={0} | all-to-all | bytes 917504 | tf_op jit(solution)/shard_map/all_to_all | solution.py:67
  257.3 2.2 fusion
  259.6 19.9 %all_to_all.33 = f32[2,896,256]{1,2,0:T(8,128)} all-to-all(f32[2,896,256]{1,2,0:T(8,128)S(1)} %bitcast.59), channel_id=1, replica_groups=mesh['sub_0'=4,'sub_1'=4,'sub_2'=4,'sub_3'=2,'panel'=2] {'panel'}, dimensions={0} | all-to-all | bytes 3670016 | tf_op jit(solution)/shard_map/all_to_all | solution.py:37
  279.5 2.5 reduce_sum.147
  282.0 2.4 fusion.4
  284.4 11.5 %all_to_all.34 = f32[2,1024,128]{1,2,0:T(8,128)} all-to-all(f32[2,1024,128]{1,2,0:T(8,128)S(1)} %bitcast.67), channel_id=1, replica_groups=mesh['sub_0'=4,'sub_1'=4,'sub_2'=4,'sub_3'=2,'panel'=2] {'panel'}, dimensions={0} | all-to-all | bytes 2097152 | tf_op jit(solution)/shard_map/all_to_all | solution.py:37
  295.9 2.2 reduce_sum.148
  300.1 2.6 gather_fusion.8
  302.7 2.7 gather_fusion.7
  305.4 14.1 %collective-permute-start.6 = (f32[384,128]{1,0:T(8,128)}, f32[384,128]{1,0:T(8,128)S(1)}, u32[]{:S(2)}, u32[]{:S(2)}) collective-permute-start(f32[384,128]{1,0:T(8,128)} %gather_fusion.7), channel_id=1, source_target_pairs={{0,2},{2,4},{4,6},{6,8},{8,10},{10,12},{12,14},{14,16},{16,18},{18... | collective-permute-start | bytes 589832 | tf_op jit(solution)/shard_map/ppermute | solution.py:20
  319.5 3.0 collective-permute-done.6
  322.5 5.1 %collective-permute-done.7 = f32[384,128]{1,0:T(8,128)S(1)} collective-permute-done((f32[384,128]{1,0:T(8,128)}, f32[384,128]{1,0:T(8,128)S(1)}, u32[]{:S(2)}, u32[]{:S(2)}) %collective-permute-start.7) | collective-permute-done | bytes 196640 | tf_op jit(solution)/shard_map/ppermute | solution.py:22
  327.5 2.3 maximum_maximum_fusion.1
  329.9 55.6 %gather_fusion.9 = f32[16384,128]{1,0:T(8,128)} fusion(f32[1793,128]{1,0:T(8,128)} %maximum_maximum_fusion.1, s32[16384]{0:T(1024)S(1)} %copy-done.7), kind=kCustom, calls=%fused_computation.9 | custom fusion | bytes 16842752 | tf_op jit(solution)/shard_map/gather | solution.py:57
  385.5 5.4 %multiply_reduce_fusion = f32[1024,128]{1,0:T(8,128)S(1)} fusion(f32[16,1024,128]{2,1,0:T(8,128)} %bitcast.56, f32[16,1024]{1,0:T(8,128)S(1)} %get-tuple-element.49), kind=kLoop, calls=%fused_computation.10 | loop fusion | flops 4063232 | bytes 8978432 | tf_op jit(solution)/shard_map/reduce_sum | solution.py:57
  391.9 8.2 %all-reduce.4 = (f32[128]{0:T(128)S(1)}, f32[128]{0:T(128)S(1)}, f32[128]{0:T(128)S(1)}, f32[128]{0:T(128)S(1)}) all-reduce(f32[128]{0:T(128)S(1)} %get-tuple-element.8, f32[128]{0:T(128)S(1)} %get-tuple-element.6, f32[128]{0:T(128)S(1)} %get-tuple-element.7, ...), channel_id=1, replica_groups=mesh['sub_0'=4,'sub_1'=4,'sub_2'=4,'sub_3'=2,'panel'=2] {'sub_0'}, use_global_device_ids=true, to_apply=%region_33.34 | all-reduce | flops 512 | bytes 4096 | tf_op jit(solution)/shard_map/psum | solution.py:42
  400.1 6.0 %all-reduce.2 = (f32[128]{0:T(128)S(1)}, f32[128]{0:T(128)S(1)}, f32[128]{0:T(128)S(1)}, f32[128]{0:T(128)S(1)}) all-reduce(f32[128]{0:T(128)S(1)} %get-tuple-element.28, f32[128]{0:T(128)S(1)} %get-tuple-element.29, f32[128]{0:T(128)S(1)} %get-tuple-element.30, ...), channel_id=1, replica_groups=mesh['sub_0'=4,'sub_1'=4,'sub_2'=4,'sub_3'=2,'panel'=2] {'sub_1'}, use_global_device_ids=true, to_apply=%region_34.35 | all-reduce | flops 512 | bytes 4096 | tf_op jit(solution)/shard_map/psum | solution.py:42
  406.1 12.3 %all-reduce = (f32[128]{0:T(128)S(1)}, f32[128]{0:T(128)S(1)}, f32[128]{0:T(128)S(1)}, f32[128]{0:T(128)S(1)}) all-reduce(f32[128]{0:T(128)S(1)} %get-tuple-element.21, f32[128]{0:T(128)S(1)} %get-tuple-element.22, f32[128]{0:T(128)S(1)} %get-tuple-element.23, ...), channel_id=1, replica_groups=mesh['sub_0'=4,'sub_1'=4,'sub_2'=4,'sub_3'=2,'panel'=2] {'sub_2'}, use_global_device_ids=true, to_apply=%region_35.36 | all-reduce | flops 512 | bytes 4096 | tf_op jit(solution)/shard_map/psum | solution.py:42
  418.4 4.3 %all-reduce.6 = (f32[128]{0:T(128)S(1)}, f32[128]{0:T(128)S(1)}, f32[128]{0:T(128)S(1)}, f32[128]{0:T(128)S(1)}) all-reduce(f32[128]{0:T(128)S(1)} %get-tuple-element.14, f32[128]{0:T(128)S(1)} %get-tuple-element.15, f32[128]{0:T(128)S(1)} %get-tuple-element.16, ...), channel_id=1, replica_groups=mesh['sub_0'=4,'sub_1'=4,'sub_2'=4,'sub_3'=2,'panel'=2] {'sub_3'}, use_global_device_ids=true, to_apply=%region_36.37 | all-reduce | flops 512 | bytes 4096 | tf_op jit(solution)/shard_map/psum | solution.py:42
  423.2 2.8 multiply_subtract_fusion
  (73 shorter events, 26.5 us)
Async XLA Ops:
  0.6 66.0 %copy-start = (bf16[1,1792,896]{2,1,0:T(8,128)(2,1)S(1)}, bf16[1,1792,896]{2,1,0:T(8,128)(2,1)}, u32[]{:S(2)}) copy-start(bf16[1,1792,896]{2,1,0:T(8,128)(2,1)} %param.22) | copy-start | bytes 9633796
  41.9 22.7 %copy-start.16 = (f32[128]{0:T(128)}, f32[128]{0:T(128)S(1)}, u32[]{:S(2)}) copy-start(f32[128]{0:T(128)S(1)} %psum.227) | copy-start | bytes 1540
  46.7 2.4 collective-permute-start
  46.9 64.0 %copy-start.10 = (s32[1024]{0:T(1024)}, s32[1024]{0:T(1024)S(1)}, u32[]{:S(2)}) copy-start(s32[1024]{0:T(1024)S(1)} %pad_clamp_fusion) | copy-start | bytes 12292
  48.8 6.6 %collective-permute-start.1 = (bf16[384,128]{1,0:T(8,128)(2,1)}, bf16[384,128]{1,0:T(8,128)(2,1)S(1)}, u32[]{:S(2)}, u32[]{:S(2)}) collective-permute-start(bf16[384,128]{1,0:T(8,128)(2,1)} %gather_fusion.1), channel_id=1, source_target_pairs={{2,0},{4,2},{6,4},{8,6},{10,8},{12,10},{14,12},{16,14},{18,16},{20... | collective-permute-start | bytes 294920 | tf_op jit(solution)/shard_map/ppermute | solution.py:22
  90.6 7.9 %copy-start.8 = (s32[16,1024]{1,0:T(8,128)S(1)}, s32[16,1024]{1,0:T(8,128)}, u32[]{:S(2)}) copy-start(s32[16,1024]{1,0:T(8,128)} %param.24) | copy-start | bytes 196612
  94.0 12.7 %all-to-all-start.2 = ((f32[2,1024,128]{1,2,0:T(8,128)}), f32[2,1024,128]{1,2,0:T(8,128)}, u32[]{:S(2)}, u32[]{:S(2)}) async-start(f32[2,1024,128]{1,2,0:T(8,128)} %bitcast.66), calls=%async_computation.2 | async-start | bytes 2097152 | tf_op jit(solution)/shard_map/all_to_all | solution.py:37
  98.5 30.2 %copy-start.9 = (f32[16,1024]{1,0:T(8,128)S(1)}, f32[16,1024]{1,0:T(8,128)}, u32[]{:S(2)}) copy-start(f32[16,1024]{1,0:T(8,128)} %param.25) | copy-start | bytes 196612
  98.5 40.1 %copy-start.6 = (s32[16384]{0:T(1024)}, s32[16384]{0:T(1024)S(1)}, u32[]{:S(2)}) copy-start(s32[16384]{0:T(1024)S(1)} %broadcast_clamp_fusion) | copy-start | bytes 196612
  98.6 30.2 %copy-start.14 = (f32[1024]{0:T(1024)S(1)}, f32[1024]{0:T(1024)}, u32[]{:S(2)}) copy-start(f32[1024]{0:T(1024)} %param.26) | copy-start | bytes 12292
  116.3 17.5 %collective-permute-start.2 = (f32[384,128]{1,0:T(8,128)}, f32[384,128]{1,0:T(8,128)S(1)}, u32[]{:S(2)}, u32[]{:S(2)}) collective-permute-start(f32[384,128]{1,0:T(8,128)} %gather_fusion.2), channel_id=1, source_target_pairs={{0,2},{2,4},{4,6},{6,8},{8,10},{10,12},{12,14},{14,16},{16,18},{18... | collective-permute-start | bytes 589832 | tf_op jit(solution)/shard_map/ppermute | solution.py:20
  128.7 7.6 %collective-permute-start.3 = (f32[384,128]{1,0:T(8,128)}, f32[384,128]{1,0:T(8,128)S(1)}, u32[]{:S(2)}, u32[]{:S(2)}) collective-permute-start(f32[384,128]{1,0:T(8,128)} %gather_fusion.3), channel_id=1, source_target_pairs={{2,0},{4,2},{6,4},{8,6},{10,8},{12,10},{14,12},{16,14},{18,16},{20... | collective-permute-start | bytes 589832 | tf_op jit(solution)/shard_map/ppermute | solution.py:22
  194.2 5.3 %copy-start.1 = (f32[1024,128]{1,0:T(8,128)S(1)}, f32[1024,128]{1,0:T(8,128)}, u32[]{:S(2)}) copy-start(f32[1024,128]{1,0:T(8,128)} %copy.24) | copy-start | bytes 1572868
  194.2 5.4 %copy-start.4 = (f32[1024,128]{1,0:T(8,128)S(1)}, f32[1024,128]{1,0:T(8,128)}, u32[]{:S(2)}) copy-start(f32[1024,128]{1,0:T(8,128)} %param.16) | copy-start | bytes 1572868
  194.2 37.4 %copy-start.17 = (f32[128]{0:T(128)S(1)}, f32[128]{0:T(128)}, u32[]{:S(2)}) copy-start(f32[128]{0:T(128)} %copy-done.16) | copy-start | bytes 1540
  231.6 0.5 copy-start.12
  239.7 3.1 collective-permute-start.4
  240.8 6.2 %collective-permute-start.5 = (bf16[384,128]{1,0:T(8,128)(2,1)}, bf16[384,128]{1,0:T(8,128)(2,1)S(1)}, u32[]{:S(2)}, u32[]{:S(2)}) collective-permute-start(bf16[384,128]{1,0:T(8,128)(2,1)} %gather_fusion.6), channel_id=1, source_target_pairs={{2,0},{4,2},{6,4},{8,6},{10,8},{12,10},{14,12},{16,14},{18,16},{20... | collective-permute-start | bytes 294920 | tf_op jit(solution)/shard_map/ppermute | solution.py:22
  284.4 15.7 %copy-start.11 = (s32[1024]{0:T(1024)S(1)}, s32[1024]{0:T(1024)}, u32[]{:S(2)}) copy-start(s32[1024]{0:T(1024)} %copy-done.10) | copy-start | bytes 12292
  298.0 31.9 %copy-start.7 = (s32[16384]{0:T(1024)S(1)}, s32[16384]{0:T(1024)}, u32[]{:S(2)}) copy-start(s32[16384]{0:T(1024)} %copy-done.6) | copy-start | bytes 196612
  305.4 17.1 %collective-permute-start.6 = (f32[384,128]{1,0:T(8,128)}, f32[384,128]{1,0:T(8,128)S(1)}, u32[]{:S(2)}, u32[]{:S(2)}) collective-permute-start(f32[384,128]{1,0:T(8,128)} %gather_fusion.7), channel_id=1, source_target_pairs={{0,2},{2,4},{4,6},{6,8},{8,10},{10,12},{12,14},{14,16},{16,18},{18... | collective-permute-start | bytes 589832 | tf_op jit(solution)/shard_map/ppermute | solution.py:20
  319.5 8.0 %collective-permute-start.7 = (f32[384,128]{1,0:T(8,128)}, f32[384,128]{1,0:T(8,128)S(1)}, u32[]{:S(2)}, u32[]{:S(2)}) collective-permute-start(f32[384,128]{1,0:T(8,128)} %gather_fusion.8), channel_id=1, source_target_pairs={{2,0},{4,2},{6,4},{8,6},{10,8},{12,10},{14,12},{16,14},{18,16},{20... | collective-permute-start | bytes 589832 | tf_op jit(solution)/shard_map/ppermute | solution.py:22
  385.5 5.4 %copy-start.2 = (f32[1024,128]{1,0:T(8,128)S(1)}, f32[1024,128]{1,0:T(8,128)}, u32[]{:S(2)}) copy-start(f32[1024,128]{1,0:T(8,128)} %copy.32) | copy-start | bytes 1572868
  385.5 5.4 %copy-start.3 = (f32[1024,128]{1,0:T(8,128)S(1)}, f32[1024,128]{1,0:T(8,128)}, u32[]{:S(2)}) copy-start(f32[1024,128]{1,0:T(8,128)} %get-tuple-element.46) | copy-start | bytes 1572868
  385.5 5.4 %copy-start.5 = (f32[1024,128]{1,0:T(8,128)S(1)}, f32[1024,128]{1,0:T(8,128)}, u32[]{:S(2)}) copy-start(f32[1024,128]{1,0:T(8,128)} %param.16) | copy-start | bytes 1572868
  385.5 37.8 %copy-start.13 = (f32[128]{0:T(128)S(1)}, f32[128]{0:T(128)}, u32[]{:S(2)}) copy-start(f32[128]{0:T(128)} %copy-done.12) | copy-start | bytes 1540
  423.2 2.8 copy-start.15
